TPU v7x, 512 devices: a whole 4x8x8 slice. The times are simulated.
512 devices in a mesh: row: 16 (over z, core), col: 32 (over x, y).
Axes of the slice: x: 4, y: 8, z: 8, core: 2. Of those that a mesh axis runs over, the one named last changes fastest.
Arguments:
- strip: float32 [20480, 128], P('row'), may hold values from -6 to 6
- block_below: float32 [64, 64], replicated, may hold values from -1 to 1
- inverse_first: float32 [64, 64], replicated, may hold values from -0.5 to 1.5, as said below
- inverse_second: float32 [64, 64], replicated, may hold values from -0.5 to 1.5, as said below
- cotangent: float32 [20480, 20480], P('row', 'col'), may hold values from -0.0390625 to 0.0390625
Outputs:
- strip_grad: float32 [20480, 128], P('row')
Inputs may be any that keep to these rules, and one draw needn't show every extreme that they name: inverse_first is lower triangular with its diagonal in 0.5 to 1.5. inverse_second is lower triangular with its diagonal in 0.5 to 1.5.
All inputs are finite; a program needn't handle non-finite values.
Results may differ from a plain program's by a relative error of at most 0.00007.
Values sent between devices are 32-bit elements; how exact they have to be, the bound alone decides.
A program may use at most 64 MiB of HBM per device.

v0:
```python
import jax
import jax.numpy as jnp
from jax import lax
from jax.sharding import PartitionSpec as P


def from_root(value, axis, source):
    kept = jnp.where(lax.axis_index(axis) == source, value, 0).astype(value.dtype)
    return lax.psum(kept, axis)


def mul(left, right):
    return jnp.dot(left, right, precision=lax.Precision.HIGHEST, preferred_element_type=jnp.float32)


def finish(bar_sum, left_block, inverse_first, inverse_second, panel):
    bar_updated = mul(-bar_sum[:, panel:], inverse_second)
    bar_first = -bar_sum[:, :panel] - mul(bar_updated, left_block)
    return jnp.concatenate([mul(bar_first, inverse_first), bar_updated], axis=1)


def shards(strip, block_below, inverse_first, inverse_second, cotangent):
    panel = inverse_first.shape[0]
    cols_here = cotangent.shape[1]
    ratio = lax.axis_size("col") // lax.axis_size("row")
    col_id = lax.axis_index("col")
    owner = col_id // ratio
    offset = col_id % ratio * cols_here
    lower_first = mul(strip[:, :panel], inverse_first.T)
    left_block = mul(block_below, inverse_first.T)
    updated = strip[:, panel:] - mul(lower_first, left_block.T)
    col_first = from_root(lax.dynamic_slice_in_dim(lower_first, offset, cols_here, 0), "row", owner)
    lower_second = mul(updated, inverse_second.T)
    col_second = from_root(
        lax.dynamic_slice_in_dim(lower_second, offset, cols_here, 0), "row", owner
    )
    col_lower = jnp.concatenate([col_first, col_second], axis=1)
    lower = jnp.concatenate([lower_first, lower_second], axis=1)
    transposed = lax.dot_general(
        cotangent,
        lower,
        (((0,), (0,)), ((), ())),
        precision=lax.Precision.HIGHEST,
        preferred_element_type=jnp.float32,
    )
    col_total = lax.psum(transposed, "row")
    row_index = lax.axis_index("row")
    pieces = []
    for member in range(ratio):
        pieces.append(from_root(col_total, "col", row_index * ratio + member))
    routed = jnp.concatenate(pieces, axis=0)
    local_sum = mul(cotangent, col_lower)
    row_total = lax.psum(local_sum, "col")
    row_total = row_total + routed
    return finish(row_total, left_block, inverse_first, inverse_second, panel)


def solution(mesh):
    return jax.shard_map(
        shards,
        mesh=mesh,
        in_specs=(P("row", None), P(), P(), P(), P("row", "col")),
        out_specs=P("row", None),
        check_vma=False,
    )
```

profile of v0, /device:TPU:64, one launch (start us, length us, event | category | flops | bytes accessed | tf_op | source)
XLA Modules:
  0.0 320.7 jit_solution(9730919756724847951)
XLA Ops:
  6.5 0.0 copy-start
  6.5 0.0 all-reduce.7.cloned.1.call-start
  6.5 1.1 fusion.11
  7.7 2.7 fusion.3
  10.3 0.0 copy-start.1
  10.3 2.5 convolution_subtract_fusion
  12.8 1.6 fusion.12
  14.5 0.0 copy-done
  14.5 3.8 %convolution_bitcast_fusion.1 = f32[640,128]{0,1:T(8,128)} fusion(f32[1280,640]{1,0:T(8,128)S(1)} %copy-done, f32[1280,64]{0,1:T(8,128)S(1)} %fusion.12, f32[1280,64]{0,1:T(8,128)} %fusion.3), kind=kOutput, calls=%fused_computation.3 | convolution fusion | flops 1258455040 | bytes 4259840 | tf_op jit(solution)/shard_map/dot_general | solution.py:39
  18.3 0.0 copy-done.1
  18.3 0.7 dynamic-slice_select_fusion
  19.1 0.0 all-reduce.7.cloned.1.call-update
  19.1 0.0 all-reduce.5.cloned.1.call-start
  19.1 118.0 %all-reduce.7.cloned.1.call-done = (f32[640,64]{0,1:T(8,128)}, f32[640,64]{0,1:T(8,128)}, f32[640,128]{0,1:T(8,128)}) async-done(((f32[640,64]{0,1:T(8,128)}, f32[640,64]{0,1:T(8,128)}, f32[640,128]{0,1:T(8,128)}), (f32[640,64]{0,1:T(8,128)}, f32[640,64]{0,1:T(8,128)}, f32[640,128]{0,1:T(8,128)})) %all-reduce.7.cloned.1.call-update) | async-done | bytes 655376 | tf_op jit(solution)/shard_map/psum | solution.py:9
  137.2 0.0 copy-start.2
  137.2 0.0 copy-start.4
  137.2 5.3 %convolution_bitcast_fusion = f32[1280,128]{0,1:T(8,128)} fusion(f32[1280,640]{1,0:T(8,128)S(1)} %copy-done, f32[640,64]{0,1:T(8,128)} %get-tuple-element.8, f32[640,64]{0,1:T(8,128)} %get-tuple-element.9), kind=kOutput, calls=%fused_computation.1 | convolution fusion | flops 1258373120 | bytes 4259840 | tf_op jit(solution)/shard_map/dot_general | solution.py:13
  142.5 0.0 copy-start.3
  142.5 0.0 copy-done.2
  142.5 0.9 broadcast_select_fusion.1
  143.4 0.0 all-reduce.5.cloned.1.call-update
  143.4 164.6 %all-reduce.5.cloned.1.call-done = (f32[1280,128]{0,1:T(8,128)}, f32[640,128]{0,1:T(8,128)}, f32[640,128]{0,1:T(8,128)}) async-done(((f32[1280,128]{0,1:T(8,128)}, f32[640,128]{0,1:T(8,128)}, f32[640,128]{0,1:T(8,128)}), (f32[1280,128]{0,1:T(8,128)}, f32[640,128]{0,1:T(8,128)}, f32[640,128]{0,1:T(8,128)})) %all-reduce.5.cloned.1.call-update) | async-done | bytes 1310736 | tf_op jit(solution)/shard_map/psum | solution.py:53
  308.0 1.3 maximum_add_fusion
  309.3 0.0 copy-done.4
  309.4 0.5 fusion.5
  309.8 0.5 convolution_subtract_fusion.1
  310.3 0.0 copy-done.3
  310.3 0.5 fusion.13
  310.8 0.9 pad_maximum_fusion
  311.7 2.2 copy.6
Async XLA Ops:
  6.5 7.9 %copy-start = (f32[1280,640]{1,0:T(8,128)S(1)}, f32[1280,640]{1,0:T(8,128)}, u32[]{:S(2)}) copy-start(f32[1280,640]{1,0:T(8,128)} %param.9) | copy-start | bytes 9830404
  6.5 130.6 %all-reduce.7.cloned.1.call-start = ((), (), s32[]{:S(2)}) async-start(), calls=%async_computation.1 | async-start | bytes 1310720 | tf_op jit(solution)/shard_map/psum | solution.py:9
  10.3 8.0 %copy-start.1 = (f32[1280,64]{0,1:T(8,128)S(1)}, f32[1280,64]{0,1:T(8,128)}, u32[]{:S(2)}) copy-start(f32[1280,64]{0,1:T(8,128)} %fusion.3) | copy-start | bytes 983044
  19.1 288.9 %all-reduce.5.cloned.1.call-start = ((), (), s32[]{:S(2)}) async-start(), calls=%async_computation | async-start | bytes 2621440 | tf_op jit(solution)/shard_map/psum | solution.py:53
  137.2 5.3 %copy-start.2 = (f32[640,128]{0,1:T(8,128)S(1)}, f32[640,128]{0,1:T(8,128)}, u32[]{:S(2)}) copy-start(f32[640,128]{0,1:T(8,128)} %get-tuple-element.10) | copy-start | bytes 983044
  137.2 172.2 %copy-start.4 = (f32[64,64]{1,0:T(8,128)S(1)}, f32[64,64]{1,0:T(8,128)}, u32[]{:S(2)}) copy-start(f32[64,64]{1,0:T(8,128)} %param.8) | copy-start | bytes 49156
  142.5 167.8 %copy-start.3 = (f32[64,64]{1,0:T(8,128)S(1)}, f32[64,64]{1,0:T(8,128)}, u32[]{:S(2)}) copy-start(f32[64,64]{1,0:T(8,128)} %param.7) | copy-start | bytes 49156
Sparse Core Ops, SparseCore 0:
  19.2 117.9 all-reduce.6
  143.5 164.4 all-reduce.4
where the time goes:
time: 321 us
  waiting for transfers between devices  283 us (88%)
  matrix products  18.5 us (6%)
  between operations  13.5 us (4%)
  other arithmetic  3.85 us (1%)
    psum x1, waiting for transfers between devices, shards(): row_total = lax.psum(local_sum, 'col')  165 us
    psum x1, waiting for transfers between devices, from_root(): return lax.psum(kept, axis)  118 us
    dot_general x8, matrix products, mul(): jnp.dot(left, right, precision=lax.Precision.HIGHEST, preferred_element_t...  14.6 us
  transfers between devices with their start and end apart: 2, of which 2 were waited for; matrix products, arithmetic and copies ran while one was open for 0% of the time, Pallas kernels for 0%

commit v1 on v0

--- a/solution.py
+++ b/solution.py
@@ -50,7 +50,11 @@
         pieces.append(from_root(col_total, "col", row_index * ratio + member))
     routed = jnp.concatenate(pieces, axis=0)
     local_sum = mul(cotangent, col_lower)
-    row_total = lax.psum(local_sum, "col")
+    row_total = local_sum
+    for hop in (1, 2, 4, 8, 16):
+        row_total = row_total + lax.ppermute(
+            row_total, "col", [(dev, dev ^ hop) for dev in range(32)]
+        )
     row_total = row_total + routed
     return finish(row_total, left_block, inverse_first, inverse_second, panel)
 

time: 321 us -> 411 us (1.28)
  waiting for transfers between devices: 283 us -> 345 us
  starting transfers between devices: 0.04 us -> 23.6 us
  other arithmetic: 3.85 us -> 8.34 us
    ppermute x0 -> x5, waiting for transfers between devices: none -> 85.3 us  [shards(): lax.ppermute(row_total, 'col', [(dev, dev ^ hop) for dev in range(32)])]
    psum x1, waiting for transfers between devices: 165 us -> 118 us  [shards(): col_total = lax.psum(transposed, 'row')]
    ppermute x0 -> x5, starting transfers between devices: none -> 23.5 us  [shards(): lax.ppermute(row_total, 'col', [(dev, dev ^ hop) for dev in range(32)])]
    psum x1, waiting for transfers between devices: 118 us -> 142 us  [from_root(): return lax.psum(kept, axis)]
  transfers between devices with their start and end apart: 2 -> 7, of which waited for: 2 -> 6; matrix products, arithmetic and copies ran while one was open for 0% -> 1% of each run, Pallas kernels for 0% -> 0%
where the time goes in v1:
time: 411 us; the launch traced here: 410 us
  waiting for transfers between devices  345 us (84%)
  starting transfers between devices  23.6 us (6%)
  matrix products  17.6 us (4%)
  between operations  13.5 us (3%)
  other arithmetic  8.34 us (2%)
    psum x1, waiting for transfers between devices, from_root(): return lax.psum(kept, axis)  142 us
    psum x1, waiting for transfers between devices, shards(): col_total = lax.psum(transposed, 'row')  118 us
    ppermute x5, waiting for transfers between devices, shards(): lax.ppermute(row_total, 'col', [(dev, dev ^ hop) for dev in range(32)])  85.3 us
    ppermute x5, starting transfers between devices, shards(): lax.ppermute(row_total, 'col', [(dev, dev ^ hop) for dev in range(32)])  23.5 us
    dot_general x8, matrix products, mul(): jnp.dot(left, right, precision=lax.Precision.HIGHEST, preferred_element_t...  13.7 us
  transfers between devices with their start and end apart: 7, of which 6 were waited for; matrix products, arithmetic and copies ran while one was open for 1% of the time, Pallas kernels for 0%

profile of v1, /device:TPU:64, one launch (start us, length us, event | category | flops | bytes accessed | tf_op | source)
XLA Modules:
  0.0 410.2 jit_solution(18251166452339789202)
XLA Ops:
  6.5 0.0 copy-start
  6.5 0.0 all-reduce.7.cloned.1.call-start
  6.5 1.1 fusion.14
  7.7 2.7 fusion.3
  10.3 0.0 copy-start.1
  10.3 2.5 convolution_subtract_fusion
  12.8 1.6 fusion.15
  14.5 0.0 copy-done
  14.5 3.8 convolution_bitcast_fusion.1
  18.3 0.0 copy-done.1
  18.3 0.7 dynamic-slice_select_fusion
  19.0 0.0 all-reduce.7.cloned.1.call-update
  19.0 0.0 all-reduce.5.cloned.1.call-start
  19.1 118.2 %all-reduce.7.cloned.1.call-done = (f32[640,128]{0,1:T(8,128)}, f32[640,64]{0,1:T(8,128)}, f32[640,64]{0,1:T(8,128)}) async-done(((f32[640,128]{0,1:T(8,128)}, f32[640,64]{0,1:T(8,128)}, f32[640,64]{0,1:T(8,128)}), (f32[640,128]{0,1:T(8,128)}, f32[640,64]{0,1:T(8,128)}, f32[640,64]{0,1:T(8,128)})) %all-reduce.7.cloned.1.call-update) | async-done | bytes 655376 | tf_op jit(solution)/shard_map/psum | solution.py:46
  137.3 4.4 %convolution_bitcast_fusion = f32[1280,128]{0,1:T(8,128)S(1)} fusion(f32[1280,640]{1,0:T(8,128)S(1)} %copy-done, f32[640,64]{0,1:T(8,128)} %get-tuple-element.8, f32[640,64]{0,1:T(8,128)} %get-tuple-element.9), kind=kOutput, calls=%fused_computation.1 | convolution fusion | flops 1258373120 | bytes 4259840 | tf_op jit(solution)/shard_map/dot_general | solution.py:13
  141.7 3.4 collective-permute-start
  145.1 15.3 %collective-permute-done = f32[1280,128]{0,1:T(8,128)S(1)} collective-permute-done((f32[1280,128]{0,1:T(8,128)S(1)}, f32[1280,128]{0,1:T(8,128)S(1)}, u32[]{:S(2)}, u32[]{:S(2)}) %collective-permute-start) | collective-permute-done | bytes 655392 | tf_op jit(solution)/shard_map/ppermute | solution.py:55
  160.4 0.1 add.42
  160.5 4.3 %collective-permute-start.1 = (f32[1280,128]{0,1:T(8,128)S(1)}, f32[1280,128]{0,1:T(8,128)S(1)}, u32[]{:S(2)}, u32[]{:S(2)}) collective-permute-start(f32[1280,128]{0,1:T(8,128)S(1)} %add.42), channel_id=1, source_target_pairs={{0,2},{1,3},{2,0},{3,1},{4,6},{5,7},{6,4},{7,5},{8,10},{9,11},{10,... | collective-permute-start | bytes 1966088 | tf_op jit(solution)/shard_map/ppermute | solution.py:55
  164.8 28.5 %collective-permute-done.1 = f32[1280,128]{0,1:T(8,128)S(1)} collective-permute-done((f32[1280,128]{0,1:T(8,128)S(1)}, f32[1280,128]{0,1:T(8,128)S(1)}, u32[]{:S(2)}, u32[]{:S(2)}) %collective-permute-start.1) | collective-permute-done | bytes 655392 | tf_op jit(solution)/shard_map/ppermute | solution.py:55
  193.3 0.1 add.43
  193.3 7.4 %collective-permute-start.2 = (f32[1280,128]{0,1:T(8,128)S(1)}, f32[1280,128]{0,1:T(8,128)S(1)}, u32[]{:S(2)}, u32[]{:S(2)}) collective-permute-start(f32[1280,128]{0,1:T(8,128)S(1)} %add.43), channel_id=1, source_target_pairs={{0,4},{1,5},{2,6},{3,7},{4,0},{5,1},{6,2},{7,3},{8,12},{9,13},{10,... | collective-permute-start | bytes 1966088 | tf_op jit(solution)/shard_map/ppermute | solution.py:55
  200.7 29.2 %collective-permute-done.2 = f32[1280,128]{0,1:T(8,128)S(1)} collective-permute-done((f32[1280,128]{0,1:T(8,128)S(1)}, f32[1280,128]{0,1:T(8,128)S(1)}, u32[]{:S(2)}, u32[]{:S(2)}) %collective-permute-start.2) | collective-permute-done | bytes 655392 | tf_op jit(solution)/shard_map/ppermute | solution.py:55
  229.9 0.9 add.44
  230.8 0.0 copy-start.3
  230.8 3.5 collective-permute-start.3
  234.3 1.9 broadcast_select_fusion.1
  236.2 0.0 copy-start.2
  236.2 0.0 all-reduce.5.cloned.1.call-update
  236.2 12.4 %collective-permute-done.3 = f32[1280,128]{0,1:T(8,128)} collective-permute-done((f32[1280,128]{0,1:T(8,128)}, f32[1280,128]{0,1:T(8,128)}, u32[]{:S(2)}, u32[]{:S(2)}) %collective-permute-start.3) | collective-permute-done | bytes 655392 | tf_op jit(solution)/shard_map/ppermute | solution.py:55
  248.6 2.2 add.45
  250.8 4.9 %collective-permute-start.4 = (f32[1280,128]{0,1:T(8,128)}, f32[1280,128]{0,1:T(8,128)}, u32[]{:S(2)}, u32[]{:S(2)}) collective-permute-start(f32[1280,128]{0,1:T(8,128)} %add.45), channel_id=1, source_target_pairs={{0,16},{1,17},{2,18},{3,19},{4,20},{5,21},{6,22},{7,23},{8,24},{9,... | collective-permute-start | bytes 1966088 | tf_op jit(solution)/shard_map/ppermute | solution.py:55
  255.8 141.5 %all-reduce.5.cloned.1.call-done = (f32[640,128]{0,1:T(8,128)}, f32[640,128]{0,1:T(8,128)}) async-done(((f32[640,128]{0,1:T(8,128)}, f32[640,128]{0,1:T(8,128)}), (f32[640,128]{0,1:T(8,128)}, f32[640,128]{0,1:T(8,128)})) %all-reduce.5.cloned.1.call-update) | async-done | bytes 655376 | tf_op jit(solution)/shard_map/psum | solution.py:9
  397.3 0.0 collective-permute-done.4
  397.3 1.6 maximum_add_fusion
  398.8 0.0 copy-done.3
  398.9 0.5 fusion.5
  399.3 0.5 fusion.16
  399.8 0.0 copy-done.2
  399.8 0.5 fusion.7
  400.3 0.9 pad_maximum_fusion
  401.2 2.2 copy.6
Async XLA Ops:
  6.5 7.9 %copy-start = (f32[1280,640]{1,0:T(8,128)S(1)}, f32[1280,640]{1,0:T(8,128)}, u32[]{:S(2)}) copy-start(f32[1280,640]{1,0:T(8,128)} %param.9) | copy-start | bytes 9830404
  6.5 130.8 %all-reduce.7.cloned.1.call-start = ((), (), s32[]{:S(2)}) async-start(), calls=%async_computation.1 | async-start | bytes 1310720 | tf_op jit(solution)/shard_map/psum | solution.py:46
  10.3 8.0 %copy-start.1 = (f32[1280,64]{0,1:T(8,128)S(1)}, f32[1280,64]{0,1:T(8,128)}, u32[]{:S(2)}) copy-start(f32[1280,64]{0,1:T(8,128)} %fusion.3) | copy-start | bytes 983044
  19.0 378.2 %all-reduce.5.cloned.1.call-start = ((), (), s32[]{:S(2)}) async-start(), calls=%async_computation | async-start | bytes 1310720 | tf_op jit(solution)/shard_map/psum | solution.py:9
  141.7 18.7 %collective-permute-start = (f32[1280,128]{0,1:T(8,128)S(1)}, f32[1280,128]{0,1:T(8,128)S(1)}, u32[]{:S(2)}, u32[]{:S(2)}) collective-permute-start(f32[1280,128]{0,1:T(8,128)S(1)} %convolution_bitcast_fusion), channel_id=1, source_target_pairs={{0,1},{1,0},{2,3},{3,2},{4,5},{5,4},{6,7},{7,6},{8,9},{9,8},{10,11... | collective-permute-start | bytes 1966088 | tf_op jit(solution)/shard_map/ppermute | solution.py:55
  160.5 32.8 %collective-permute-start.1 = (f32[1280,128]{0,1:T(8,128)S(1)}, f32[1280,128]{0,1:T(8,128)S(1)}, u32[]{:S(2)}, u32[]{:S(2)}) collective-permute-start(f32[1280,128]{0,1:T(8,128)S(1)} %add.42), channel_id=1, source_target_pairs={{0,2},{1,3},{2,0},{3,1},{4,6},{5,7},{6,4},{7,5},{8,10},{9,11},{10,... | collective-permute-start | bytes 1966088 | tf_op jit(solution)/shard_map/ppermute | solution.py:55
  193.3 36.5 %collective-permute-start.2 = (f32[1280,128]{0,1:T(8,128)S(1)}, f32[1280,128]{0,1:T(8,128)S(1)}, u32[]{:S(2)}, u32[]{:S(2)}) collective-permute-start(f32[1280,128]{0,1:T(8,128)S(1)} %add.43), channel_id=1, source_target_pairs={{0,4},{1,5},{2,6},{3,7},{4,0},{5,1},{6,2},{7,3},{8,12},{9,13},{10,... | collective-permute-start | bytes 1966088 | tf_op jit(solution)/shard_map/ppermute | solution.py:55
  230.8 168.1 %copy-start.3 = (f32[64,64]{1,0:T(8,128)S(1)}, f32[64,64]{1,0:T(8,128)}, u32[]{:S(2)}) copy-start(f32[64,64]{1,0:T(8,128)} %param.8) | copy-start | bytes 49156
  230.8 17.8 %collective-permute-start.3 = (f32[1280,128]{0,1:T(8,128)}, f32[1280,128]{0,1:T(8,128)}, u32[]{:S(2)}, u32[]{:S(2)}) collective-permute-start(f32[1280,128]{0,1:T(8,128)} %add.44), channel_id=1, source_target_pairs={{0,8},{1,9},{2,10},{3,11},{4,12},{5,13},{6,14},{7,15},{8,0},{9,1},... | collective-permute-start | bytes 1966088 | tf_op jit(solution)/shard_map/ppermute | solution.py:55
  236.2 163.6 %copy-start.2 = (f32[64,64]{1,0:T(8,128)S(1)}, f32[64,64]{1,0:T(8,128)}, u32[]{:S(2)}) copy-start(f32[64,64]{1,0:T(8,128)} %param.7) | copy-start | bytes 49156
  250.8 146.5 %collective-permute-start.4 = (f32[1280,128]{0,1:T(8,128)}, f32[1280,128]{0,1:T(8,128)}, u32[]{:S(2)}, u32[]{:S(2)}) collective-permute-start(f32[1280,128]{0,1:T(8,128)} %add.45), channel_id=1, source_target_pairs={{0,16},{1,17},{2,18},{3,19},{4,20},{5,21},{6,22},{7,23},{8,24},{9,... | collective-permute-start | bytes 1966088 | tf_op jit(solution)/shard_map/ppermute | solution.py:55
Sparse Core Ops, SparseCore 0:
  19.2 118.0 all-reduce.6
  236.4 160.8 all-reduce.4
